TPU v7x, 32 devices: a whole 2x2x4 slice. The times are simulated.
32 devices in a mesh: ens: 2 (over x), band: 16 (over z, y, core).
Axes of the slice: x: 2, y: 2, z: 4, core: 2. Of those that a mesh axis runs over, the one named last changes fastest.
Arguments:
- atm_state: bfloat16 [256, 128, 384], P(('ens', 'band')), parts along dimension 0, may hold values from -6 to 6
- ocean_state: bfloat16 [256, 128, 384], P(('ens', 'band')), parts along dimension 0, may hold values from -6 to 6
- dw_kernel: float32 [2, 7, 7, 384], replicated, may hold values from -0.875 to 0.875
- norm_gain: float32 [2, 384], replicated, may hold values from 0.1 to 1.9
- w_up: bfloat16 [2, 384, 1536], replicated, may hold values from -0.3125 to 0.3125
- b_up: float32 [2, 1536], replicated, may hold values from -3 to 3
- w_down: bfloat16 [2, 384, 1536], replicated, may hold values from -0.15625 to 0.15625
- flux_out: bfloat16 [384, 256], replicated, may hold values from -0.3125 to 0.3125
- flux_in: bfloat16 [256, 384], replicated, may hold values from -0.375 to 0.375
- partner: int32 [32], P('ens'), parts along dimension 0, may hold values from 0 to 15, each once
- remap: int32 [256], P('ens'), parts along dimension 0, may hold values from 0 to 7
- land_mask: int32 [256, 128], P(('ens', 'band')), parts along dimension 0, may hold values 0 or 1
Outputs:
- atm_next: bfloat16 [256, 128, 384], P(('ens', 'band')), parts along dimension 0
- ocean_next: bfloat16 [256, 128, 384], P(('ens', 'band')), parts along dimension 0
There are 2 independent parts, one for each index of `ens`. A program takes and returns all parts, laid end to end along the dimension named above; an argument that names none is the same for every part. Nothing has to cross between parts.
Inputs may be any that keep to these rules, and one draw needn't show every extreme that they name: Each of the 16 atmosphere bands is the partner of exactly one ocean band.
All inputs are finite; a program needn't handle non-finite values. No bound on the sum of `land_mask` on one device may be relied on, other than what follows from the above.
Results may differ from a plain program's by a relative error of at most 0.0075.
Values may be sent and summed in bfloat16 or wider, within the bound.
No kernel may reach another device: no remote copies, remote signals or barrier semaphores. Data moves between devices by JAX's collectives and lax.ppermute only.
A program may use at most 64 MiB of HBM per device.

v0:
```python
import jax
import jax.numpy as jnp
from jax import lax
from jax.sharding import PartitionSpec as P


def with_halo(array, sides, width):
    for axis, dim in sides:
        size, length = (lax.axis_size(axis), array.shape[dim])
        up = [(i, (i + 1) % size) for i in range(size - 1)]
        down = [(j, i) for i, j in up]
        last = lax.slice_in_dim(array, length - width, length, axis=dim)
        first = lax.slice_in_dim(array, 0, width, axis=dim)
        before = lax.ppermute(last, axis, up)
        after = lax.ppermute(first, axis, down)
        array = jnp.concatenate([before, array, after], axis=dim)
    return array


def conv_norm(field, kernel, gain):
    padded = with_halo(field, (("band", 0),), 3)
    padded = jnp.concatenate([padded[:, -3:], padded, padded[:, :3]], axis=1).astype(jnp.float32)
    height, width = (field.shape[0], field.shape[1])
    total = jnp.zeros(field.shape, jnp.float32)
    for a in range(7):
        for b in range(7):
            total = total + kernel[a, b] * padded[a : a + height, b : b + width]
    center = jnp.mean(total, axis=-1, keepdims=True)
    spread = jnp.mean((total - center) ** 2, axis=-1, keepdims=True)
    normed = ((total - center) * lax.rsqrt(spread + 1e-06) * gain).astype(jnp.bfloat16)
    return normed.reshape(height * width, field.shape[2])


def mixer(field, which, dw_kernel, norm_gain, w_up, b_up, w_down):
    normed = conv_norm(field, dw_kernel[which], norm_gain[which])
    hidden = jax.nn.gelu(
        jnp.dot(normed, w_up[which], preferred_element_type=jnp.float32) + b_up[which],
        approximate=True,
    ).astype(jnp.bfloat16)
    update = lax.dot_general(
        hidden, w_down[which], (((1,), (1,)), ((), ())), preferred_element_type=jnp.float32
    )
    return (field.astype(jnp.float32) + update.reshape(field.shape)).astype(jnp.bfloat16)


def partner_move(tile, indices):
    picked = jnp.take(
        lax.all_to_all(tile, "band", split_axis=1, concat_axis=0, tiled=True), indices, axis=0
    )
    return lax.all_to_all(picked, "band", split_axis=0, concat_axis=1, tiled=True)


def per_device(
    atm_state,
    ocean_state,
    dw_kernel,
    norm_gain,
    w_up,
    b_up,
    w_down,
    flux_out,
    flux_in,
    partner,
    remap,
    land_mask,
):
    atm_next = mixer(atm_state, 0, dw_kernel, norm_gain, w_up, b_up, w_down)
    height, width, channels = atm_next.shape
    band_rows = remap.shape[0] // partner.shape[0]
    indices = jnp.repeat(partner, band_rows) * band_rows + remap
    surface = jnp.dot(
        atm_next.reshape(-1, channels), flux_out, preferred_element_type=jnp.float32
    ).astype(jnp.bfloat16)
    moved = partner_move(surface.reshape(height, width, -1), indices).reshape(height * width, -1)
    forcing = jnp.dot(moved, flux_in, preferred_element_type=jnp.float32).reshape(
        height, width, channels
    )
    ocean_in = (
        ocean_state.astype(jnp.float32) + land_mask.astype(jnp.float32)[:, :, None] * forcing
    ).astype(jnp.bfloat16)
    ocean_next = mixer(ocean_in, 1, dw_kernel, norm_gain, w_up, b_up, w_down)
    return (atm_next, ocean_next)


def solution(mesh):
    in_specs = (
        P(("ens", "band"), None, None),
        P(("ens", "band"), None, None),
        P(),
        P(),
        P(),
        P(),
        P(),
        P(),
        P(),
        P("ens"),
        P("ens"),
        P(("ens", "band"), None),
    )
    out_specs = (P(("ens", "band"), None, None), P(("ens", "band"), None, None))
    return jax.shard_map(
        per_device, mesh=mesh, in_specs=in_specs, out_specs=out_specs, check_vma=False
    )
```

profile of v0, /device:TPU:13, one launch (start us, length us, event | category | flops | bytes accessed | tf_op | source)
XLA Modules:
  0.0 111.3 jit_solution(1870685209608916670)
XLA Ops:
  0.7 1.2 %fusion.132 = (bf16[3,128,384]{2,1,0:T(8,128)(2,1)S(1)}, bf16[3,128,384]{2,1,0:T(8,128)(2,1)S(1)}) fusion(bf16[8,128,384]{2,1,0:T(8,128)(2,1)} %param.12), kind=kLoop, calls=%fused_computation.360 | loop fusion | bytes 1179648 | tf_op jit(solution)/shard_map/slice | solution.py:13
  1.9 2.6 %collective-permute-start.1 = (bf16[3,128,384]{2,1,0:T(8,128)(2,1)S(1)}, bf16[3,128,384]{2,1,0:T(8,128)(2,1)S(1)}, u32[]{:S(2)}, u32[]{:S(2)}) collective-permute-start(bf16[3,128,384]{2,1,0:T(8,128)(2,1)S(1)} %get-tuple-element.114), channel_id=1, source_target_pairs={{1,0},{2,1},{3,2},{4,3},{5,4},{6,5},{7,6},{8,7},{9,8},{10,9},{11,1... | collective-permute-start | bytes 884744 | tf_op jit(solution)/shard_map/ppermute | solution.py:15
  4.5 3.9 %collective-permute-start = (bf16[3,128,384]{2,1,0:T(8,128)(2,1)S(1)}, bf16[3,128,384]{2,1,0:T(8,128)(2,1)S(1)}, u32[]{:S(2)}, u32[]{:S(2)}) collective-permute-start(bf16[3,128,384]{2,1,0:T(8,128)(2,1)S(1)} %get-tuple-element.115), channel_id=1, source_target_pairs={{0,1},{1,2},{2,3},{3,4},{4,5},{5,6},{6,7},{7,8},{8,9},{9,10},{10,1... | collective-permute-start | bytes 884744 | tf_op jit(solution)/shard_map/ppermute | solution.py:14
  8.3 1.1 %fusion.133 = (f32[1,7,7,384]{3,0,2,1:T(1,128)S(1)}, f32[1,7,7,384]{3,0,2,1:T(1,128)S(1)}) fusion(f32[2,7,7,384]{3,0,2,1:T(2,128)} %param.14), kind=kLoop, calls=%fused_computation.361 | loop fusion | bytes 301056 | tf_op jit(solution)/shard_map/slice | solution.py:35
  9.9 2.1 %collective-permute-done = bf16[3,128,384]{2,1,0:T(8,128)(2,1)S(1)} collective-permute-done((bf16[3,128,384]{2,1,0:T(8,128)(2,1)S(1)}, bf16[3,128,384]{2,1,0:T(8,128)(2,1)S(1)}, u32[]{:S(2)}, u32[]{:S(2)}) %collective-permute-start) | collective-permute-done | bytes 294944 | tf_op jit(solution)/shard_map/ppermute | solution.py:14
  12.3 0.3 maximum_convert_fusion
  12.6 12.0 %fusion.128 = (f32[8,128]{1,0:T(8,128)S(1)}, f32[8,128,384]{2,1,0:T(8,128)}) fusion(f32[14,134,384]{2,1,0:T(8,128)S(1)} %maximum_convert_fusion, f32[384]{0:T(512)S(1)} %get-tuple-element.52, f32[384]{0:T(512)S(1)} %get-tuple-element.53, f32[384]{0:T(512)S(1)} %get-tuple-element.54, f32[384]{0:T(512)S(1)} %get-tuple-element.55, ...), kind=kLoop, calls=%fused_computation.357 | loop fusion | flops 38534144 | bytes 78722560 | tf_op jit(solution)/shard_map/reduce_sum | solution.py:28
  24.6 1.9 %multiply_reduce_fusion.1 = f32[8,128]{1,0:T(8,128)S(1)} fusion(f32[8,128,384]{2,1,0:T(8,128)} %get-tuple-element.109, f32[8,128]{1,0:T(8,128)S(1)} %broadcast_multiply_fusion.1), kind=kLoop, calls=%fused_computation.219 | loop fusion | flops 1178624 | bytes 1581056 | tf_op jit(solution)/shard_map/reduce_sum | solution.py:29
  26.6 0.3 multiply_convert_fusion.1
  26.9 1.3 %copy-done.13 = bf16[2,384,1536]{2,1,0:T(8,128)(2,1)S(1)} copy-done((bf16[2,384,1536]{2,1,0:T(8,128)(2,1)S(1)}, bf16[2,384,1536]{2,1,0:T(8,128)(2,1)}, u32[]{:S(2)}) %copy-start.13) | copy-done | bytes 2359320
  28.2 2.9 %fusion.7 = bf16[1024,1536]{1,0:T(8,128)(2,1)S(1)} fusion(bf16[1024,384]{1,0:T(8,128)(2,1)S(1)} %bitcast.48, f32[1536]{0:T(1024)S(1)} %get-tuple-element.101, bf16[2,384,1536]{2,1,0:T(8,128)(2,1)S(1)} %copy-done.13), kind=kOutput, calls=%fused_computation.10 | convolution fusion | flops 1223688192 | bytes 5120000 | tf_op jit(solution)/shard_map/dot_general | solution.py:37
  31.1 1.8 %add_convert_fusion.2 = bf16[8,128,384]{2,1,0:T(8,128)(2,1)S(1)} fusion(bf16[8,128,384]{2,1,0:T(8,128)(2,1)S(1)} %copy-done.6, bf16[8,128,1536]{2,1,0:T(8,128)(2,1)S(1)} %bitcast.51, bf16[2,384,1536]{2,1,0:T(8,128)(2,1)S(1)} %copy-done.15), kind=kOutput, calls=%fused_computation.217 | convolution fusion | flops 1209139200 | bytes 5898240 | tf_op jit(solution)/shard_map/dot_general | solution.py:40
  33.0 0.9 copy-done.7
  33.8 0.4 convolution_convert_fusion
  34.3 1.1 copy.22
  35.4 7.5 %all-to-all-start = ((bf16[8,128,256]{2,0,1:T(8,128)(2,1)}), bf16[8,128,256]{2,0,1:T(8,128)(2,1)S(1)}, u32[]{:S(2)}, u32[]{:S(2)}) async-start(bf16[8,128,256]{2,0,1:T(8,128)(2,1)} %copy.22), calls=%async_computation | async-start | bytes 1048576 | tf_op jit(solution)/shard_map/all_to_all | solution.py:48
  43.1 13.4 %all-to-all-done = bf16[8,128,256]{2,0,1:T(8,128)(2,1)S(1)} async-done(((bf16[8,128,256]{2,0,1:T(8,128)(2,1)}), bf16[8,128,256]{2,0,1:T(8,128)(2,1)S(1)}, u32[]{:S(2)}, u32[]{:S(2)}) %all-to-all-start) | async-done | bytes 524320 | tf_op jit(solution)/shard_map/all_to_all | solution.py:48
  56.6 0.6 gather_fusion
  57.2 1.0 broadcast_select_fusion
  58.2 4.9 %all-to-all-start.1 = ((bf16[128,8,256]{2,1,0:T(8,128)(2,1)}), bf16[128,8,256]{2,1,0:T(8,128)(2,1)S(1)}, u32[]{:S(2)}, u32[]{:S(2)}) async-start(bf16[128,8,256]{2,1,0:T(8,128)(2,1)} %broadcast_select_fusion), calls=%async_computation.1 | async-start | bytes 1048576 | tf_op jit(solution)/shard_map/all_to_all | solution.py:50
  63.1 13.6 %all-to-all-done.1 = bf16[128,8,256]{2,1,0:T(8,128)(2,1)S(1)} async-done(((bf16[128,8,256]{2,1,0:T(8,128)(2,1)}), bf16[128,8,256]{2,1,0:T(8,128)(2,1)S(1)}, u32[]{:S(2)}, u32[]{:S(2)}) %all-to-all-start.1) | async-done | bytes 524320 | tf_op jit(solution)/shard_map/all_to_all | solution.py:50
  76.7 0.4 add_convert_fusion.1
  77.2 3.7 %collective-permute-start.2 = (bf16[3,128,384]{2,1,0:T(8,128)(2,1)S(1)}, bf16[3,128,384]{2,1,0:T(8,128)(2,1)S(1)}, u32[]{:S(2)}, u32[]{:S(2)}) collective-permute-start(bf16[3,128,384]{2,1,0:T(8,128)(2,1)S(1)} %get-tuple-element.112), channel_id=1, source_target_pairs={{0,1},{1,2},{2,3},{3,4},{4,5},{5,6},{6,7},{7,8},{8,9},{9,10},{10,1... | collective-permute-start | bytes 884744 | tf_op jit(solution)/shard_map/ppermute | solution.py:14
  80.9 2.1 %collective-permute-start.3 = (bf16[3,128,384]{2,1,0:T(8,128)(2,1)S(1)}, bf16[3,128,384]{2,1,0:T(8,128)(2,1)S(1)}, u32[]{:S(2)}, u32[]{:S(2)}) collective-permute-start(bf16[3,128,384]{2,1,0:T(8,128)(2,1)S(1)} %get-tuple-element.113), channel_id=1, source_target_pairs={{1,0},{2,1},{3,2},{4,3},{5,4},{6,5},{7,6},{8,7},{9,8},{10,9},{11,1... | collective-permute-start | bytes 884744 | tf_op jit(solution)/shard_map/ppermute | solution.py:15
  83.2 1.3 %collective-permute-done.2 = bf16[3,128,384]{2,1,0:T(8,128)(2,1)S(1)} collective-permute-done((bf16[3,128,384]{2,1,0:T(8,128)(2,1)S(1)}, bf16[3,128,384]{2,1,0:T(8,128)(2,1)S(1)}, u32[]{:S(2)}, u32[]{:S(2)}) %collective-permute-start.2) | collective-permute-done | bytes 294944 | tf_op jit(solution)/shard_map/ppermute | solution.py:14
  84.6 5.3 %collective-permute-done.3 = bf16[3,128,384]{2,1,0:T(8,128)(2,1)S(1)} collective-permute-done((bf16[3,128,384]{2,1,0:T(8,128)(2,1)S(1)}, bf16[3,128,384]{2,1,0:T(8,128)(2,1)S(1)}, u32[]{:S(2)}, u32[]{:S(2)}) %collective-permute-start.3) | collective-permute-done | bytes 294944 | tf_op jit(solution)/shard_map/ppermute | solution.py:15
  90.2 12.0 %fusion.126 = (f32[8,128]{1,0:T(8,128)S(1)}, f32[8,128,384]{2,1,0:T(8,128)}) fusion(f32[14,134,384]{2,1,0:T(8,128)S(1)} %fusion.113, f32[384]{0:T(512)S(1)} %get-tuple-element.3, f32[384]{0:T(512)S(1)} %get-tuple-element.4, f32[384]{0:T(512)S(1)} %get-tuple-element.5, f32[384]{0:T(512)S(1)} %get-tuple-element.6, f32[384]{0:T(512)S(1)} %get-tuple-element.7, ...), kind=kLoop, calls=%fused_computation.356 | loop fusion | flops 38534144 | bytes 78722560 | tf_op jit(solution)/shard_map/reduce_sum | solution.py:28
  102.1 1.9 %multiply_reduce_fusion = f32[8,128]{1,0:T(8,128)S(1)} fusion(f32[8,128,384]{2,1,0:T(8,128)} %get-tuple-element.105, f32[8,128]{1,0:T(8,128)S(1)} %broadcast_multiply_fusion), kind=kLoop, calls=%fused_computation.215 | loop fusion | flops 1178624 | bytes 1581056 | tf_op jit(solution)/shard_map/reduce_sum | solution.py:29
  104.1 0.3 multiply_convert_fusion
  104.4 1.3 %copy-done.14 = bf16[2,384,1536]{2,1,0:T(8,128)(2,1)S(1)} copy-done((bf16[2,384,1536]{2,1,0:T(8,128)(2,1)S(1)}, bf16[2,384,1536]{2,1,0:T(8,128)(2,1)}, u32[]{:S(2)}) %copy-start.14) | copy-done | bytes 2359320
  105.7 2.9 %fusion.15 = bf16[1024,1536]{1,0:T(8,128)(2,1)S(1)} fusion(bf16[1024,384]{1,0:T(8,128)(2,1)S(1)} %bitcast.47, f32[1536]{0:T(1024)S(1)} %get-tuple-element.100, bf16[2,384,1536]{2,1,0:T(8,128)(2,1)S(1)} %copy-done.14), kind=kOutput, calls=%fused_computation.18 | convolution fusion | flops 1223688192 | bytes 5120000 | tf_op jit(solution)/shard_map/dot_general | solution.py:37
  108.6 2.7 %add_convert_fusion = bf16[8,128,384]{2,1,0:T(8,128)(2,1)} fusion(bf16[8,128,384]{2,1,0:T(8,128)(2,1)S(1)} %copy-done.4, bf16[8,128,1536]{2,1,0:T(8,128)(2,1)S(1)} %bitcast.50, bf16[2,384,1536]{2,1,0:T(8,128)(2,1)S(1)} %copy-done.16), kind=kOutput, calls=%fused_computation.213 | convolution fusion | flops 1209139200 | bytes 5898240 | tf_op jit(solution)/shard_map/dot_general | solution.py:40
  (62 shorter events, 1.7 us)
Async XLA Ops:
  0.6 76.0 %copy-start = (bf16[256,384]{1,0:T(8,128)(2,1)S(1)}, bf16[256,384]{1,0:T(8,128)(2,1)}, u32[]{:S(2)}) copy-start(bf16[256,384]{1,0:T(8,128)(2,1)} %param.20) | copy-start | bytes 589828
  0.6 11.4 %copy-start.5 = (bf16[8,128,384]{2,1,0:T(8,128)(2,1)S(1)}, bf16[8,128,384]{2,1,0:T(8,128)(2,1)}, u32[]{:S(2)}) copy-start(bf16[8,128,384]{2,1,0:T(8,128)(2,1)} %param.12) | copy-start | bytes 2359300
  0.7 9.0 %copy-start.9 = (f32[2,1536]{1,0:T(2,128)S(1)}, f32[2,1536]{1,0:T(2,128)}, u32[]{:S(2)}) copy-start(f32[2,1536]{1,0:T(2,128)} %param.17) | copy-start | bytes 36868
  0.7 9.2 %copy-start.11 = (f32[2,384]{1,0:T(2,128)S(1)}, f32[2,384]{1,0:T(2,128)}, u32[]{:S(2)}) copy-start(f32[2,384]{1,0:T(2,128)} %param.15) | copy-start | bytes 9220
  1.9 10.3 %collective-permute-start.1 = (bf16[3,128,384]{2,1,0:T(8,128)(2,1)S(1)}, bf16[3,128,384]{2,1,0:T(8,128)(2,1)S(1)}, u32[]{:S(2)}, u32[]{:S(2)}) collective-permute-start(bf16[3,128,384]{2,1,0:T(8,128)(2,1)S(1)} %get-tuple-element.114), channel_id=1, source_target_pairs={{1,0},{2,1},{3,2},{4,3},{5,4},{6,5},{7,6},{8,7},{9,8},{10,9},{11,1... | collective-permute-start | bytes 884744 | tf_op jit(solution)/shard_map/ppermute | solution.py:15
  4.5 7.5 %collective-permute-start = (bf16[3,128,384]{2,1,0:T(8,128)(2,1)S(1)}, bf16[3,128,384]{2,1,0:T(8,128)(2,1)S(1)}, u32[]{:S(2)}, u32[]{:S(2)}) collective-permute-start(bf16[3,128,384]{2,1,0:T(8,128)(2,1)S(1)} %get-tuple-element.115), channel_id=1, source_target_pairs={{0,1},{1,2},{2,3},{3,4},{4,5},{5,6},{6,7},{7,8},{8,9},{9,10},{10,1... | collective-permute-start | bytes 884744 | tf_op jit(solution)/shard_map/ppermute | solution.py:14
  24.6 1.9 %copy-start.2 = (f32[8,128,384]{2,1,0:T(8,128)S(1)}, f32[8,128,384]{2,1,0:T(8,128)}, u32[]{:S(2)}) copy-start(f32[8,128,384]{2,1,0:T(8,128)} %get-tuple-element.109) | copy-start | bytes 4718596
  26.5 1.7 %copy-start.13 = (bf16[2,384,1536]{2,1,0:T(8,128)(2,1)S(1)}, bf16[2,384,1536]{2,1,0:T(8,128)(2,1)}, u32[]{:S(2)}) copy-start(bf16[2,384,1536]{2,1,0:T(8,128)(2,1)} %param.16) | copy-start | bytes 7077892
  28.2 2.9 %copy-start.6 = (bf16[8,128,384]{2,1,0:T(8,128)(2,1)S(1)}, bf16[8,128,384]{2,1,0:T(8,128)(2,1)}, u32[]{:S(2)}) copy-start(bf16[8,128,384]{2,1,0:T(8,128)(2,1)} %param.12) | copy-start | bytes 2359300
  28.2 2.9 %copy-start.15 = (bf16[2,384,1536]{2,1,0:T(8,128)(2,1)S(1)}, bf16[2,384,1536]{2,1,0:T(8,128)(2,1)}, u32[]{:S(2)}) copy-start(bf16[2,384,1536]{2,1,0:T(8,128)(2,1)} %param.18) | copy-start | bytes 7077892
  31.1 2.7 %copy-start.8 = (bf16[384,256]{1,0:T(8,128)(2,1)S(1)}, bf16[384,256]{1,0:T(8,128)(2,1)}, u32[]{:S(2)}) copy-start(bf16[384,256]{1,0:T(8,128)(2,1)} %param.19) | copy-start | bytes 589828
  32.9 0.9 copy-start.7
  33.8 9.0 %copy-start.18 = (s32[16]{0:T(128)S(1)}, s32[16]{0:T(128)}, u32[]{:S(2)}) copy-start(s32[16]{0:T(128)} %param.21) | copy-start | bytes 196
  33.8 9.2 %copy-start.12 = (s32[128]{0:T(128)S(1)}, s32[128]{0:T(128)}, u32[]{:S(2)}) copy-start(s32[128]{0:T(128)} %param.22) | copy-start | bytes 1540
  35.4 21.1 %all-to-all-start = ((bf16[8,128,256]{2,0,1:T(8,128)(2,1)}), bf16[8,128,256]{2,0,1:T(8,128)(2,1)S(1)}, u32[]{:S(2)}, u32[]{:S(2)}) async-start(bf16[8,128,256]{2,0,1:T(8,128)(2,1)} %copy.22), calls=%async_computation | async-start | bytes 1048576 | tf_op jit(solution)/shard_map/all_to_all | solution.py:48
  56.5 6.5 %copy-start.10 = (s32[8,128]{1,0:T(8,128)S(1)}, s32[8,128]{1,0:T(8,128)}, u32[]{:S(2)}) copy-start(s32[8,128]{1,0:T(8,128)} %param.23) | copy-start | bytes 12292
  56.6 20.1 %copy-start.17 = (bf16[8,128,384]{2,1,0:T(8,128)(2,1)S(1)}, bf16[8,128,384]{2,1,0:T(8,128)(2,1)}, u32[]{:S(2)}) copy-start(bf16[8,128,384]{2,1,0:T(8,128)(2,1)} %param.13) | copy-start | bytes 2359300
  58.2 18.4 %all-to-all-start.1 = ((bf16[128,8,256]{2,1,0:T(8,128)(2,1)}), bf16[128,8,256]{2,1,0:T(8,128)(2,1)S(1)}, u32[]{:S(2)}, u32[]{:S(2)}) async-start(bf16[128,8,256]{2,1,0:T(8,128)(2,1)} %broadcast_select_fusion), calls=%async_computation.1 | async-start | bytes 1048576 | tf_op jit(solution)/shard_map/all_to_all | solution.py:50
  77.1 13.0 %copy-start.3 = (bf16[8,128,384]{2,1,0:T(8,128)(2,1)}, bf16[8,128,384]{2,1,0:T(8,128)(2,1)S(1)}, u32[]{:S(2)}) copy-start(bf16[8,128,384]{2,1,0:T(8,128)(2,1)S(1)} %add_convert_fusion.1) | copy-start | bytes 2359300
  77.2 7.4 %collective-permute-start.2 = (bf16[3,128,384]{2,1,0:T(8,128)(2,1)S(1)}, bf16[3,128,384]{2,1,0:T(8,128)(2,1)S(1)}, u32[]{:S(2)}, u32[]{:S(2)}) collective-permute-start(bf16[3,128,384]{2,1,0:T(8,128)(2,1)S(1)} %get-tuple-element.112), channel_id=1, source_target_pairs={{0,1},{1,2},{2,3},{3,4},{4,5},{5,6},{6,7},{7,8},{8,9},{9,10},{10,1... | collective-permute-start | bytes 884744 | tf_op jit(solution)/shard_map/ppermute | solution.py:14
  80.9 8.9 %collective-permute-start.3 = (bf16[3,128,384]{2,1,0:T(8,128)(2,1)S(1)}, bf16[3,128,384]{2,1,0:T(8,128)(2,1)S(1)}, u32[]{:S(2)}, u32[]{:S(2)}) collective-permute-start(bf16[3,128,384]{2,1,0:T(8,128)(2,1)S(1)} %get-tuple-element.113), channel_id=1, source_target_pairs={{1,0},{2,1},{3,2},{4,3},{5,4},{6,5},{7,6},{8,7},{9,8},{10,9},{11,1... | collective-permute-start | bytes 884744 | tf_op jit(solution)/shard_map/ppermute | solution.py:15
  102.1 1.9 %copy-start.1 = (f32[8,128,384]{2,1,0:T(8,128)S(1)}, f32[8,128,384]{2,1,0:T(8,128)}, u32[]{:S(2)}) copy-start(f32[8,128,384]{2,1,0:T(8,128)} %get-tuple-element.105) | copy-start | bytes 4718596
  104.0 1.7 %copy-start.14 = (bf16[2,384,1536]{2,1,0:T(8,128)(2,1)S(1)}, bf16[2,384,1536]{2,1,0:T(8,128)(2,1)}, u32[]{:S(2)}) copy-start(bf16[2,384,1536]{2,1,0:T(8,128)(2,1)} %param.16) | copy-start | bytes 7077892
  105.7 2.9 %copy-start.4 = (bf16[8,128,384]{2,1,0:T(8,128)(2,1)S(1)}, bf16[8,128,384]{2,1,0:T(8,128)(2,1)}, u32[]{:S(2)}) copy-start(bf16[8,128,384]{2,1,0:T(8,128)(2,1)} %copy-done.3) | copy-start | bytes 2359300
  105.7 2.9 %copy-start.16 = (bf16[2,384,1536]{2,1,0:T(8,128)(2,1)S(1)}, bf16[2,384,1536]{2,1,0:T(8,128)(2,1)}, u32[]{:S(2)}) copy-start(bf16[2,384,1536]{2,1,0:T(8,128)(2,1)} %param.18) | copy-start | bytes 7077892
where the time goes:
time: 112 us; the launch traced here: 111 us
  waiting for transfers between devices  35.6 us (32%)
  other arithmetic  30.1 us (27%)
  starting transfers between devices  24.6 us (22%)
  matrix products  11.2 us (10%)
  local copies, waits for them, and re-layouts  8.78 us (8%)
    reduce_sum x2, other arithmetic, conv_norm(): center = jnp.mean(total, axis=-1, keepdims=True)  23.9 us
    all_to_all x1, waiting for transfers between devices, partner_move(): lax.all_to_all(picked, 'band', split_axis=0, concat_axis=1, tiled=True)  13.6 us
    all_to_all x1, waiting for transfers between devices, partner_move(): lax.all_to_all(tile, 'band', split_axis=1, concat_axis=0, tiled=True)  13.4 us
    ppermute x2, starting transfers between devices, with_halo(): before = lax.ppermute(last, axis, up)  7.54 us
    all_to_all x1, starting transfers between devices, partner_move(): lax.all_to_all(tile, 'band', split_axis=1, concat_axis=0, tiled=True)  7.51 us
    dot_general x2, matrix products, mixer(): jnp.dot(normed, w_up[which], preferred_element_type=jnp.float32)  5.77 us
    ppermute x2, waiting for transfers between devices, with_halo(): after = lax.ppermute(first, axis, down)  5.25 us
    all_to_all x1, starting transfers between devices, partner_move(): lax.all_to_all(picked, 'band', split_axis=0, concat_axis=1, tiled=True)  4.87 us
  transfers between devices with their start and end apart: 6, of which 5 were waited for; matrix products, arithmetic and copies ran while one was open for 2% of the time, Pallas kernels for 0%

commit v1 on v0

--- a/solution.py
+++ b/solution.py
@@ -2,6 +2,13 @@
 import jax.numpy as jnp
 from jax import lax
 from jax.sharding import PartitionSpec as P
+
+
+def stacked_exchange(array, axis, split, join):
+    devices = lax.axis_size(axis)
+    pieces = jnp.stack(jnp.split(array, devices, axis=split), axis=0)
+    pieces = lax.all_to_all(pieces, axis, split_axis=0, concat_axis=0)
+    return jnp.concatenate(pieces, axis=join)
 
 
 def with_halo(array, sides, width):
@@ -47,7 +54,7 @@
     picked = jnp.take(
         lax.all_to_all(tile, "band", split_axis=1, concat_axis=0, tiled=True), indices, axis=0
     )
-    return lax.all_to_all(picked, "band", split_axis=0, concat_axis=1, tiled=True)
+    return stacked_exchange(picked, "band", 0, 1)
 
 
 def per_device(

time: 112 us -> 121 us (1.080)
  local copies, waits for them, and re-layouts: 8.78 us -> 18.7 us
    unnamed x40 -> x55, local copies, waits for them, and re-layouts: 3.71 us -> 13 us
where the time goes in v1:
time: 121 us; the launch traced here: 120 us
  waiting for transfers between devices  35.6 us (29%)
  other arithmetic  29.3 us (24%)
  starting transfers between devices  24.6 us (20%)
  local copies, waits for them, and re-layouts  18.7 us (15%)
  matrix products  11.2 us (9%)
    reduce_sum x2, other arithmetic, conv_norm(): center = jnp.mean(total, axis=-1, keepdims=True)  23.9 us
    all_to_all x1, waiting for transfers between devices, stacked_exchange(): pieces = lax.all_to_all(pieces, axis, split_axis=0, concat_axis=0)  13.6 us
    all_to_all x1, waiting for transfers between devices, partner_move(): lax.all_to_all(tile, 'band', split_axis=1, concat_axis=0, tiled=True)  13.4 us
    unnamed x55, local copies, waits for them, and re-layouts  13 us
    ppermute x2, starting transfers between devices, with_halo(): before = lax.ppermute(last, axis, up)  7.55 us
    all_to_all x1, starting transfers between devices, partner_move(): lax.all_to_all(tile, 'band', split_axis=1, concat_axis=0, tiled=True)  7.51 us
    dot_general x2, matrix products, mixer(): jnp.dot(normed, w_up[which], preferred_element_type=jnp.float32)  5.77 us
    ppermute x2, waiting for transfers between devices, with_halo(): after = lax.ppermute(first, axis, down)  5.25 us
  transfers between devices with their start and end apart: 6, of which 5 were waited for; matrix products, arithmetic and copies ran while one was open for 2% of the time, Pallas kernels for 0%

profile of v1, /device:TPU:13, one launch (start us, length us, event | category | flops | bytes accessed | tf_op | source)
XLA Modules:
  0.0 120.4 jit_solution(7862633904614548391)
XLA Ops:
  0.7 1.2 fusion.132
  1.9 2.6 %collective-permute-start.1 = (bf16[3,128,384]{2,1,0:T(8,128)(2,1)S(1)}, bf16[3,128,384]{2,1,0:T(8,128)(2,1)S(1)}, u32[]{:S(2)}, u32[]{:S(2)}) collective-permute-start(bf16[3,128,384]{2,1,0:T(8,128)(2,1)S(1)} %get-tuple-element.114), channel_id=1, source_target_pairs={{1,0},{2,1},{3,2},{4,3},{5,4},{6,5},{7,6},{8,7},{9,8},{10,9},{11,1... | collective-permute-start | bytes 884744 | tf_op jit(solution)/shard_map/ppermute | solution.py:22
  4.5 3.9 %collective-permute-start = (bf16[3,128,384]{2,1,0:T(8,128)(2,1)S(1)}, bf16[3,128,384]{2,1,0:T(8,128)(2,1)S(1)}, u32[]{:S(2)}, u32[]{:S(2)}) collective-permute-start(bf16[3,128,384]{2,1,0:T(8,128)(2,1)S(1)} %get-tuple-element.115), channel_id=1, source_target_pairs={{0,1},{1,2},{2,3},{3,4},{4,5},{5,6},{6,7},{7,8},{8,9},{9,10},{10,1... | collective-permute-start | bytes 884744 | tf_op jit(solution)/shard_map/ppermute | solution.py:21
  8.3 1.1 fusion.133
  9.9 2.1 %collective-permute-done = bf16[3,128,384]{2,1,0:T(8,128)(2,1)S(1)} collective-permute-done((bf16[3,128,384]{2,1,0:T(8,128)(2,1)S(1)}, bf16[3,128,384]{2,1,0:T(8,128)(2,1)S(1)}, u32[]{:S(2)}, u32[]{:S(2)}) %collective-permute-start) | collective-permute-done | bytes 294944 | tf_op jit(solution)/shard_map/ppermute | solution.py:21
  12.6 12.0 %fusion.128 = (f32[8,128]{1,0:T(8,128)S(1)}, f32[8,128,384]{2,1,0:T(8,128)}) fusion(f32[14,134,384]{2,1,0:T(8,128)S(1)} %maximum_convert_fusion, f32[384]{0:T(512)S(1)} %get-tuple-element.52, f32[384]{0:T(512)S(1)} %get-tuple-element.53, f32[384]{0:T(512)S(1)} %get-tuple-element.54, f32[384]{0:T(512)S(1)} %get-tuple-element.55, ...), kind=kLoop, calls=%fused_computation.389 | loop fusion | flops 38534144 | bytes 78722560 | tf_op jit(solution)/shard_map/reduce_sum | solution.py:35
  24.6 1.9 %multiply_reduce_fusion.1 = f32[8,128]{1,0:T(8,128)S(1)} fusion(f32[8,128,384]{2,1,0:T(8,128)} %get-tuple-element.109, f32[8,128]{1,0:T(8,128)S(1)} %broadcast_multiply_fusion.1), kind=kLoop, calls=%fused_computation.219 | loop fusion | flops 1178624 | bytes 1581056 | tf_op jit(solution)/shard_map/reduce_sum | solution.py:36
  26.9 1.3 %copy-done.13 = bf16[2,384,1536]{2,1,0:T(8,128)(2,1)S(1)} copy-done((bf16[2,384,1536]{2,1,0:T(8,128)(2,1)S(1)}, bf16[2,384,1536]{2,1,0:T(8,128)(2,1)}, u32[]{:S(2)}) %copy-start.13) | copy-done | bytes 2359320
  28.2 2.9 %fusion.7 = bf16[1024,1536]{1,0:T(8,128)(2,1)S(1)} fusion(bf16[1024,384]{1,0:T(8,128)(2,1)S(1)} %bitcast.113, f32[1536]{0:T(1024)S(1)} %get-tuple-element.101, bf16[2,384,1536]{2,1,0:T(8,128)(2,1)S(1)} %copy-done.13), kind=kOutput, calls=%fused_computation.10 | convolution fusion | flops 1223688192 | bytes 5120000 | tf_op jit(solution)/shard_map/dot_general | solution.py:44
  31.1 1.8 %add_convert_fusion.2 = bf16[8,128,384]{2,1,0:T(8,128)(2,1)S(1)} fusion(bf16[8,128,384]{2,1,0:T(8,128)(2,1)S(1)} %copy-done.6, bf16[8,128,1536]{2,1,0:T(8,128)(2,1)S(1)} %bitcast.115, bf16[2,384,1536]{2,1,0:T(8,128)(2,1)S(1)} %copy-done.15), kind=kOutput, calls=%fused_computation.217 | convolution fusion | flops 1209139200 | bytes 5898240 | tf_op jit(solution)/shard_map/dot_general | solution.py:47
  33.0 0.9 copy-done.7
  34.3 1.1 copy.37
  35.4 7.5 %all-to-all-start = ((bf16[8,128,256]{2,0,1:T(8,128)(2,1)}), bf16[8,128,256]{2,0,1:T(8,128)(2,1)S(1)}, u32[]{:S(2)}, u32[]{:S(2)}) async-start(bf16[8,128,256]{2,0,1:T(8,128)(2,1)} %copy.37), calls=%async_computation | async-start | bytes 1048576 | tf_op jit(solution)/shard_map/all_to_all | solution.py:55
  43.1 13.4 %all-to-all-done = bf16[8,128,256]{2,0,1:T(8,128)(2,1)S(1)} async-done(((bf16[8,128,256]{2,0,1:T(8,128)(2,1)}), bf16[8,128,256]{2,0,1:T(8,128)(2,1)S(1)}, u32[]{:S(2)}, u32[]{:S(2)}) %all-to-all-start) | async-done | bytes 524320 | tf_op jit(solution)/shard_map/all_to_all | solution.py:55
  56.5 0.6 gather_fusion
  57.4 0.6 constant_dynamic-update-slice_fusion.18
  58.1 0.6 constant_dynamic-update-slice_fusion.17
  58.7 0.6 constant_dynamic-update-slice_fusion.16
  59.3 0.6 constant_dynamic-update-slice_fusion.15
  59.9 0.6 constant_dynamic-update-slice_fusion.14
  60.5 0.6 constant_dynamic-update-slice_fusion.13
  67.3 4.9 %all-to-all-start.1 = ((bf16[16,8,8,256]{3,2,1,0:T(8,128)(2,1)}), bf16[16,8,8,256]{3,2,1,0:T(8,128)(2,1)S(1)}, u32[]{:S(2)}, u32[]{:S(2)}) async-start(bf16[16,8,8,256]{3,2,1,0:T(8,128)(2,1)} %constant_dynamic-update-slice_fusion.3), calls=%async_computation.1 | async-start | bytes 1048576 | tf_op jit(solution)/shard_map/all_to_all | solution.py:10
  72.2 13.6 %all-to-all-done.1 = bf16[16,8,8,256]{3,2,1,0:T(8,128)(2,1)S(1)} async-done(((bf16[16,8,8,256]{3,2,1,0:T(8,128)(2,1)}), bf16[16,8,8,256]{3,2,1,0:T(8,128)(2,1)S(1)}, u32[]{:S(2)}, u32[]{:S(2)}) %all-to-all-start.1) | async-done | bytes 524320 | tf_op jit(solution)/shard_map/all_to_all | solution.py:10
  86.3 3.7 %collective-permute-start.2 = (bf16[3,128,384]{2,1,0:T(8,128)(2,1)S(1)}, bf16[3,128,384]{2,1,0:T(8,128)(2,1)S(1)}, u32[]{:S(2)}, u32[]{:S(2)}) collective-permute-start(bf16[3,128,384]{2,1,0:T(8,128)(2,1)S(1)} %get-tuple-element.112), channel_id=1, source_target_pairs={{0,1},{1,2},{2,3},{3,4},{4,5},{5,6},{6,7},{7,8},{8,9},{9,10},{10,1... | collective-permute-start | bytes 884744 | tf_op jit(solution)/shard_map/ppermute | solution.py:21
  90.0 2.1 %collective-permute-start.3 = (bf16[3,128,384]{2,1,0:T(8,128)(2,1)S(1)}, bf16[3,128,384]{2,1,0:T(8,128)(2,1)S(1)}, u32[]{:S(2)}, u32[]{:S(2)}) collective-permute-start(bf16[3,128,384]{2,1,0:T(8,128)(2,1)S(1)} %get-tuple-element.113), channel_id=1, source_target_pairs={{1,0},{2,1},{3,2},{4,3},{5,4},{6,5},{7,6},{8,7},{9,8},{10,9},{11,1... | collective-permute-start | bytes 884744 | tf_op jit(solution)/shard_map/ppermute | solution.py:22
  92.3 1.3 %collective-permute-done.2 = bf16[3,128,384]{2,1,0:T(8,128)(2,1)S(1)} collective-permute-done((bf16[3,128,384]{2,1,0:T(8,128)(2,1)S(1)}, bf16[3,128,384]{2,1,0:T(8,128)(2,1)S(1)}, u32[]{:S(2)}, u32[]{:S(2)}) %collective-permute-start.2) | collective-permute-done | bytes 294944 | tf_op jit(solution)/shard_map/ppermute | solution.py:21
  93.7 5.3 %collective-permute-done.3 = bf16[3,128,384]{2,1,0:T(8,128)(2,1)S(1)} collective-permute-done((bf16[3,128,384]{2,1,0:T(8,128)(2,1)S(1)}, bf16[3,128,384]{2,1,0:T(8,128)(2,1)S(1)}, u32[]{:S(2)}, u32[]{:S(2)}) %collective-permute-start.3) | collective-permute-done | bytes 294944 | tf_op jit(solution)/shard_map/ppermute | solution.py:22
  99.3 12.0 %fusion.126 = (f32[8,128]{1,0:T(8,128)S(1)}, f32[8,128,384]{2,1,0:T(8,128)}) fusion(f32[14,134,384]{2,1,0:T(8,128)S(1)} %fusion.113, f32[384]{0:T(512)S(1)} %get-tuple-element.3, f32[384]{0:T(512)S(1)} %get-tuple-element.4, f32[384]{0:T(512)S(1)} %get-tuple-element.5, f32[384]{0:T(512)S(1)} %get-tuple-element.6, f32[384]{0:T(512)S(1)} %get-tuple-element.7, ...), kind=kLoop, calls=%fused_computation.388 | loop fusion | flops 38534144 | bytes 78722560 | tf_op jit(solution)/shard_map/reduce_sum | solution.py:35
  111.2 1.9 %multiply_reduce_fusion = f32[8,128]{1,0:T(8,128)S(1)} fusion(f32[8,128,384]{2,1,0:T(8,128)} %get-tuple-element.105, f32[8,128]{1,0:T(8,128)S(1)} %broadcast_multiply_fusion), kind=kLoop, calls=%fused_computation.215 | loop fusion | flops 1178624 | bytes 1581056 | tf_op jit(solution)/shard_map/reduce_sum | solution.py:36
  113.5 1.3 %copy-done.14 = bf16[2,384,1536]{2,1,0:T(8,128)(2,1)S(1)} copy-done((bf16[2,384,1536]{2,1,0:T(8,128)(2,1)S(1)}, bf16[2,384,1536]{2,1,0:T(8,128)(2,1)}, u32[]{:S(2)}) %copy-start.14) | copy-done | bytes 2359320
  114.8 2.9 %fusion.15 = bf16[1024,1536]{1,0:T(8,128)(2,1)S(1)} fusion(bf16[1024,384]{1,0:T(8,128)(2,1)S(1)} %bitcast.112, f32[1536]{0:T(1024)S(1)} %get-tuple-element.100, bf16[2,384,1536]{2,1,0:T(8,128)(2,1)S(1)} %copy-done.14), kind=kOutput, calls=%fused_computation.18 | convolution fusion | flops 1223688192 | bytes 5120000 | tf_op jit(solution)/shard_map/dot_general | solution.py:44
  117.7 2.7 %add_convert_fusion = bf16[8,128,384]{2,1,0:T(8,128)(2,1)} fusion(bf16[8,128,384]{2,1,0:T(8,128)(2,1)S(1)} %copy-done.4, bf16[8,128,1536]{2,1,0:T(8,128)(2,1)S(1)} %bitcast.114, bf16[2,384,1536]{2,1,0:T(8,128)(2,1)S(1)} %copy-done.16), kind=kOutput, calls=%fused_computation.213 | convolution fusion | flops 1209139200 | bytes 5898240 | tf_op jit(solution)/shard_map/dot_general | solution.py:47
  (78 shorter events, 9.9 us)
Async XLA Ops:
  0.6 85.1 %copy-start = (bf16[256,384]{1,0:T(8,128)(2,1)S(1)}, bf16[256,384]{1,0:T(8,128)(2,1)}, u32[]{:S(2)}) copy-start(bf16[256,384]{1,0:T(8,128)(2,1)} %param.20) | copy-start | bytes 589828
  0.6 11.4 %copy-start.5 = (bf16[8,128,384]{2,1,0:T(8,128)(2,1)S(1)}, bf16[8,128,384]{2,1,0:T(8,128)(2,1)}, u32[]{:S(2)}) copy-start(bf16[8,128,384]{2,1,0:T(8,128)(2,1)} %param.12) | copy-start | bytes 2359300
  0.7 9.0 %copy-start.9 = (f32[2,1536]{1,0:T(2,128)S(1)}, f32[2,1536]{1,0:T(2,128)}, u32[]{:S(2)}) copy-start(f32[2,1536]{1,0:T(2,128)} %param.17) | copy-start | bytes 36868
  0.7 9.2 %copy-start.11 = (f32[2,384]{1,0:T(2,128)S(1)}, f32[2,384]{1,0:T(2,128)}, u32[]{:S(2)}) copy-start(f32[2,384]{1,0:T(2,128)} %param.15) | copy-start | bytes 9220
  1.9 10.3 %collective-permute-start.1 = (bf16[3,128,384]{2,1,0:T(8,128)(2,1)S(1)}, bf16[3,128,384]{2,1,0:T(8,128)(2,1)S(1)}, u32[]{:S(2)}, u32[]{:S(2)}) collective-permute-start(bf16[3,128,384]{2,1,0:T(8,128)(2,1)S(1)} %get-tuple-element.114), channel_id=1, source_target_pairs={{1,0},{2,1},{3,2},{4,3},{5,4},{6,5},{7,6},{8,7},{9,8},{10,9},{11,1... | collective-permute-start | bytes 884744 | tf_op jit(solution)/shard_map/ppermute | solution.py:22
  4.5 7.5 %collective-permute-start = (bf16[3,128,384]{2,1,0:T(8,128)(2,1)S(1)}, bf16[3,128,384]{2,1,0:T(8,128)(2,1)S(1)}, u32[]{:S(2)}, u32[]{:S(2)}) collective-permute-start(bf16[3,128,384]{2,1,0:T(8,128)(2,1)S(1)} %get-tuple-element.115), channel_id=1, source_target_pairs={{0,1},{1,2},{2,3},{3,4},{4,5},{5,6},{6,7},{7,8},{8,9},{9,10},{10,1... | collective-permute-start | bytes 884744 | tf_op jit(solution)/shard_map/ppermute | solution.py:21
  24.6 1.9 %copy-start.2 = (f32[8,128,384]{2,1,0:T(8,128)S(1)}, f32[8,128,384]{2,1,0:T(8,128)}, u32[]{:S(2)}) copy-start(f32[8,128,384]{2,1,0:T(8,128)} %get-tuple-element.109) | copy-start | bytes 4718596
  26.5 1.7 %copy-start.13 = (bf16[2,384,1536]{2,1,0:T(8,128)(2,1)S(1)}, bf16[2,384,1536]{2,1,0:T(8,128)(2,1)}, u32[]{:S(2)}) copy-start(bf16[2,384,1536]{2,1,0:T(8,128)(2,1)} %param.16) | copy-start | bytes 7077892
  28.2 2.9 %copy-start.6 = (bf16[8,128,384]{2,1,0:T(8,128)(2,1)S(1)}, bf16[8,128,384]{2,1,0:T(8,128)(2,1)}, u32[]{:S(2)}) copy-start(bf16[8,128,384]{2,1,0:T(8,128)(2,1)} %param.12) | copy-start | bytes 2359300
  28.2 2.9 %copy-start.15 = (bf16[2,384,1536]{2,1,0:T(8,128)(2,1)S(1)}, bf16[2,384,1536]{2,1,0:T(8,128)(2,1)}, u32[]{:S(2)}) copy-start(bf16[2,384,1536]{2,1,0:T(8,128)(2,1)} %param.18) | copy-start | bytes 7077892
  31.1 2.7 %copy-start.8 = (bf16[384,256]{1,0:T(8,128)(2,1)S(1)}, bf16[384,256]{1,0:T(8,128)(2,1)}, u32[]{:S(2)}) copy-start(bf16[384,256]{1,0:T(8,128)(2,1)} %param.19) | copy-start | bytes 589828
  32.9 0.9 copy-start.7
  33.8 9.0 %copy-start.18 = (s32[16]{0:T(128)S(1)}, s32[16]{0:T(128)}, u32[]{:S(2)}) copy-start(s32[16]{0:T(128)} %param.21) | copy-start | bytes 196
  33.8 9.2 %copy-start.12 = (s32[128]{0:T(128)S(1)}, s32[128]{0:T(128)}, u32[]{:S(2)}) copy-start(s32[128]{0:T(128)} %param.22) | copy-start | bytes 1540
  35.4 21.1 %all-to-all-start = ((bf16[8,128,256]{2,0,1:T(8,128)(2,1)}), bf16[8,128,256]{2,0,1:T(8,128)(2,1)S(1)}, u32[]{:S(2)}, u32[]{:S(2)}) async-start(bf16[8,128,256]{2,0,1:T(8,128)(2,1)} %copy.37), calls=%async_computation | async-start | bytes 1048576 | tf_op jit(solution)/shard_map/all_to_all | solution.py:55
  57.2 15.0 %copy-start.10 = (s32[8,128]{1,0:T(8,128)S(1)}, s32[8,128]{1,0:T(8,128)}, u32[]{:S(2)}) copy-start(s32[8,128]{1,0:T(8,128)} %param.23) | copy-start | bytes 12292
  57.2 28.5 %copy-start.17 = (bf16[8,128,384]{2,1,0:T(8,128)(2,1)S(1)}, bf16[8,128,384]{2,1,0:T(8,128)(2,1)}, u32[]{:S(2)}) copy-start(bf16[8,128,384]{2,1,0:T(8,128)(2,1)} %param.13) | copy-start | bytes 2359300
  67.3 18.4 %all-to-all-start.1 = ((bf16[16,8,8,256]{3,2,1,0:T(8,128)(2,1)}), bf16[16,8,8,256]{3,2,1,0:T(8,128)(2,1)S(1)}, u32[]{:S(2)}, u32[]{:S(2)}) async-start(bf16[16,8,8,256]{3,2,1,0:T(8,128)(2,1)} %constant_dynamic-update-slice_fusion.3), calls=%async_computation.1 | async-start | bytes 1048576 | tf_op jit(solution)/shard_map/all_to_all | solution.py:10
  86.2 13.0 %copy-start.3 = (bf16[8,128,384]{2,1,0:T(8,128)(2,1)}, bf16[8,128,384]{2,1,0:T(8,128)(2,1)S(1)}, u32[]{:S(2)}) copy-start(bf16[8,128,384]{2,1,0:T(8,128)(2,1)S(1)} %add_convert_fusion.1) | copy-start | bytes 2359300
  86.3 7.4 %collective-permute-start.2 = (bf16[3,128,384]{2,1,0:T(8,128)(2,1)S(1)}, bf16[3,128,384]{2,1,0:T(8,128)(2,1)S(1)}, u32[]{:S(2)}, u32[]{:S(2)}) collective-permute-start(bf16[3,128,384]{2,1,0:T(8,128)(2,1)S(1)} %get-tuple-element.112), channel_id=1, source_target_pairs={{0,1},{1,2},{2,3},{3,4},{4,5},{5,6},{6,7},{7,8},{8,9},{9,10},{10,1... | collective-permute-start | bytes 884744 | tf_op jit(solution)/shard_map/ppermute | solution.py:21
  90.0 8.9 %collective-permute-start.3 = (bf16[3,128,384]{2,1,0:T(8,128)(2,1)S(1)}, bf16[3,128,384]{2,1,0:T(8,128)(2,1)S(1)}, u32[]{:S(2)}, u32[]{:S(2)}) collective-permute-start(bf16[3,128,384]{2,1,0:T(8,128)(2,1)S(1)} %get-tuple-element.113), channel_id=1, source_target_pairs={{1,0},{2,1},{3,2},{4,3},{5,4},{6,5},{7,6},{8,7},{9,8},{10,9},{11,1... | collective-permute-start | bytes 884744 | tf_op jit(solution)/shard_map/ppermute | solution.py:22
  111.2 1.9 %copy-start.1 = (f32[8,128,384]{2,1,0:T(8,128)S(1)}, f32[8,128,384]{2,1,0:T(8,128)}, u32[]{:S(2)}) copy-start(f32[8,128,384]{2,1,0:T(8,128)} %get-tuple-element.105) | copy-start | bytes 4718596
  113.1 1.7 %copy-start.14 = (bf16[2,384,1536]{2,1,0:T(8,128)(2,1)S(1)}, bf16[2,384,1536]{2,1,0:T(8,128)(2,1)}, u32[]{:S(2)}) copy-start(bf16[2,384,1536]{2,1,0:T(8,128)(2,1)} %param.16) | copy-start | bytes 7077892
  114.8 2.9 %copy-start.4 = (bf16[8,128,384]{2,1,0:T(8,128)(2,1)S(1)}, bf16[8,128,384]{2,1,0:T(8,128)(2,1)}, u32[]{:S(2)}) copy-start(bf16[8,128,384]{2,1,0:T(8,128)(2,1)} %copy-done.3) | copy-start | bytes 2359300
  114.8 2.9 %copy-start.16 = (bf16[2,384,1536]{2,1,0:T(8,128)(2,1)S(1)}, bf16[2,384,1536]{2,1,0:T(8,128)(2,1)}, u32[]{:S(2)}) copy-start(bf16[2,384,1536]{2,1,0:T(8,128)(2,1)} %param.18) | copy-start | bytes 7077892
